TPU v7x, 32 devices: a whole 2x2x4 slice. The times are simulated.
32 devices in a mesh: gx: 4 (over y, x), gy: 8 (over z, core).
Axes of the slice: x: 2, y: 2, z: 4, core: 2. Of those that a mesh axis runs over, the one named last changes fastest.
Arguments:
- inputs: bfloat16 [16, 16, 32, 512], P('gx', 'gy'), may hold values from -6 to 6
- cotangent: bfloat16 [16, 16, 32, 512], P('gx', 'gy'), may hold values from -6 to 6
- point_weight: bfloat16 [32, 32], replicated, may hold values from -1 to 1
- spectral_weight: bfloat16 [2304, 24, 2048], P(('gx', 'gy')), may hold values from -0.75 to 0.75
Outputs:
- grad_input: bfloat16 [16, 16, 32, 512], P('gx', 'gy')
- grad_spectral: float32 [2304, 24, 2048], P(('gx', 'gy'))
All inputs are finite; a program needn't handle non-finite values.
Results may differ from a plain program's by a relative error of at most 0.034.
Values may be sent and summed in bfloat16 or wider, within the bound.
No kernel may reach another device: no remote copies, remote signals or barrier semaphores. Data moves between devices by JAX's collectives and lax.ppermute only.
A program may use at most 192 MiB of HBM per device.

v0:
```python
import math
import jax
import jax.numpy as jnp
from jax import lax
from jax.sharding import PartitionSpec as P

NZ = 64
NT = 8
KX = 24
KY = 24
KZ = 12
KT = 8


def kept_angles(positions, kept_count, length):
    index = jnp.arange(kept_count, dtype=jnp.int32)
    frequency = jnp.where(index < kept_count // 2, index, index - kept_count)
    turns = positions[:, None] * frequency[None, :] % length
    return turns.astype(jnp.float32) * (2.0 * math.pi / length)


def axis_tables(positions, kept_count, length):
    angles = kept_angles(positions, kept_count, length)
    return (jnp.cos(angles), jnp.sin(angles))


def depth_tables():
    angle_depth = kept_angles(jnp.arange(NZ, dtype=jnp.int32), KZ, NZ)
    angle_time = kept_angles(jnp.arange(NT, dtype=jnp.int32), KT, NT)
    angles = (angle_depth[:, None, :, None] + angle_time[None, :, None, :]).reshape(
        NZ * NT, KZ * KT
    )
    return (jnp.cos(angles), jnp.sin(angles))


def settle(values):
    return lax.optimization_barrier(values.astype(jnp.bfloat16))


def rotate(spectra, cosine_table, sine_table, pattern, turn_sign):
    half_width = spectra.shape[-1] // 2
    with_cosine = jnp.einsum(pattern, spectra, cosine_table, precision=lax.Precision.HIGHEST)
    with_sine = jnp.einsum(pattern, spectra, sine_table, precision=lax.Precision.HIGHEST)
    real_part = with_cosine[..., :half_width] + turn_sign * with_sine[..., half_width:]
    imag_part = with_cosine[..., half_width:] - turn_sign * with_sine[..., :half_width]
    return jnp.concatenate([real_part, imag_part], -1)


def depth_forward(field_in, tables, factor):
    widened = field_in.astype(jnp.float32)
    with_cosine = jnp.einsum("xycs,sk->kxyc", widened, tables[0], precision=lax.Precision.HIGHEST)
    with_sine = jnp.einsum("xycs,sk->kxyc", widened, tables[1], precision=lax.Precision.HIGHEST)
    return jnp.concatenate([with_cosine, -with_sine], -1) * factor


def depth_inverse(spectra, tables, factor):
    half_width = spectra.shape[-1] // 2
    with_cosine = jnp.einsum(
        "kxyc,sk->xycs", spectra[..., :half_width], tables[0], precision=lax.Precision.HIGHEST
    )
    with_sine = jnp.einsum(
        "kxyc,sk->xycs", spectra[..., half_width:], tables[1], precision=lax.Precision.HIGHEST
    )
    return (with_cosine - with_sine) * factor


def contract_in(left, right):
    return jnp.einsum("mkc,mkco->mko", left, right, precision=lax.Precision.HIGHEST)


def contract_out(left, right):
    return jnp.einsum("mko,mkco->mkc", left, right, precision=lax.Precision.HIGHEST)


def partial_outer(left, right):
    return jnp.einsum("mkc,mko->mkco", left, right, precision=lax.Precision.HIGHEST)


def mix_modes(spectra, weight):
    half_width = spectra.shape[-1] // 2
    weight_wide = weight.astype(jnp.float32)
    weight_real, weight_imag = (weight_wide[..., :half_width], weight_wide[..., half_width:])
    real_in, imag_in = (spectra[..., :half_width], spectra[..., half_width:])
    real_out = contract_in(real_in, weight_real) - contract_in(imag_in, weight_imag)
    imag_out = contract_in(real_in, weight_imag) + contract_in(imag_in, weight_real)
    return jnp.concatenate([real_out, imag_out], -1)


def adjoint_modes(spectra, weight):
    half_width = spectra.shape[-1] // 2
    weight_wide = weight.astype(jnp.float32)
    weight_real, weight_imag = (weight_wide[..., :half_width], weight_wide[..., half_width:])
    real_in, imag_in = (spectra[..., :half_width], spectra[..., half_width:])
    real_out = contract_out(real_in, weight_real) + contract_out(imag_in, weight_imag)
    imag_out = contract_out(imag_in, weight_real) - contract_out(real_in, weight_imag)
    return jnp.concatenate([real_out, imag_out], -1)


def weight_grad(spectra_in, spectra_back):
    half_width = spectra_in.shape[-1] // 2
    real_in, imag_in = (spectra_in[..., :half_width], spectra_in[..., half_width:])
    real_back, imag_back = (spectra_back[..., :half_width], spectra_back[..., half_width:])
    real_part = partial_outer(real_in, real_back) + partial_outer(imag_in, imag_back)
    imag_part = partial_outer(real_in, imag_back) - partial_outer(imag_in, real_back)
    return jnp.concatenate([real_part, imag_part], -1)


def exact_gelu(values):
    return jax.nn.gelu(values, approximate=False)


def per_device(inputs, cotangent, point_weight, spectral_weight):
    rows_x, rows_y, channels, cells = inputs.shape
    mode_rows, mode_cols, flat_width = spectral_weight.shape
    weight_blocks = spectral_weight.reshape(mode_rows, mode_cols, channels, 2 * channels)
    count_gx = lax.axis_size("gx")
    count_gy = lax.axis_size("gy")
    length_x = rows_x * count_gx
    length_y = rows_y * count_gy
    depth_pair = depth_tables()
    own_x = lax.axis_index("gx") * rows_x + jnp.arange(rows_x, dtype=jnp.int32)
    local_x = axis_tables(own_x, KX, length_x)
    whole_y = axis_tables(jnp.arange(length_y, dtype=jnp.int32), KY, length_y)
    total_cells = length_x * length_y * cells
    kept_total = KX * KY * KZ * KT

    def to_modes(field_in, factor):
        depth_spec = settle(depth_forward(field_in, depth_pair, factor))
        share = depth_spec.shape[0] // count_gx
        first_spectra = lax.psum_scatter(
            rotate(
                depth_spec.astype(jnp.float32), local_x[0], local_x[1], "rxyc,xk->rkyc", 1.0
            ).astype(jnp.bfloat16),
            "gx",
            scatter_dimension=0,
            tiled=True,
        ).astype(jnp.float32)
        first_spectra = settle(first_spectra).reshape(share * KX, rows_y, 2 * channels)
        arrived_modes = lax.all_to_all(first_spectra, "gy", split_axis=0, concat_axis=1, tiled=True)
        return rotate(arrived_modes.astype(jnp.float32), whole_y[0], whole_y[1], "myc,yk->mkc", 1.0)

    def to_space(spectra, factor):
        back_rows = settle(rotate(spectra, whole_y[0], whole_y[1], "mkc,yk->myc", -1.0))
        returned = lax.all_to_all(back_rows, "gy", split_axis=1, concat_axis=0, tiled=True)
        share = returned.shape[0] // KX
        returned = returned.reshape(share, KX, rows_y, 2 * channels)
        back_depth = settle(
            rotate(
                lax.all_gather(returned, "gx", axis=0, tiled=True).astype(jnp.float32),
                local_x[0],
                local_x[1],
                "rkyc,xk->rxyc",
                -1.0,
            )
        )
        return depth_inverse(back_depth.astype(jnp.float32), depth_pair, factor)

    spectra_in = to_modes(inputs, 1.0 / math.sqrt(total_cells))
    mixed = mix_modes(spectra_in, weight_blocks)
    spectral_out = to_space(mixed, 1.0 / math.sqrt(kept_total))
    pointwise = jnp.einsum(
        "xycs,co->xyos", inputs, point_weight, preferred_element_type=jnp.float32
    )
    before = spectral_out + pointwise
    unused_out, pullback = jax.vjp(exact_gelu, before)
    slope = settle(pullback(cotangent.astype(jnp.float32))[0])
    spectra_back = to_modes(slope, 1.0 / math.sqrt(kept_total))
    grad_spectral = weight_grad(spectra_in, spectra_back).reshape(mode_rows, mode_cols, flat_width)
    adjoint = adjoint_modes(spectra_back, weight_blocks)
    spectral_grad = to_space(adjoint, 1.0 / math.sqrt(total_cells))
    pointwise_grad = jnp.einsum(
        "xyos,co->xycs", slope, point_weight, preferred_element_type=jnp.float32
    )
    grad_input = (pointwise_grad + spectral_grad).astype(jnp.bfloat16)
    return (grad_input, grad_spectral)


def solution(mesh):
    placed = (
        P("gx", "gy", None, None),
        P("gx", "gy", None, None),
        P(),
        P(("gx", "gy"), None, None),
    )
    return jax.shard_map(
        per_device,
        mesh=mesh,
        in_specs=placed,
        out_specs=(P("gx", "gy", None, None), P(("gx", "gy"), None, None)),
        check_vma=False,
    )
```

profile of v0, /device:TPU:0, one launch (start us, length us, event | category | flops | bytes accessed | tf_op | source)
XLA Modules:
  0.0 453.6 jit_solution(6818993007358127799)
XLA Ops:
  7.4 12.3 %add_sine_fusion = (f32[64,8,12,8]{1,0,3,2:T(8,128)}, f32[64,8,12,8]{1,0,3,2:T(8,128)S(1)}) fusion(f32[8,8]{0,1:T(8,128)S(1)} %fusion.94, f32[64,12]{0,1:T(8,128)S(1)} %fusion.75), kind=kLoop, calls=%fused_computation.19 | loop fusion | flops 49152 | bytes 396544 | tf_op jit(solution)/shard_map/sin | solution.py:33
  19.8 3.9 reshape.129
  23.7 2.8 reshape.128
  26.5 1.3 convolution_negate_fusion.1
  27.8 1.3 fusion.52
  29.1 1.0 convolution_bitcast_fusion.2
  30.1 1.0 convolution_bitcast_fusion.3
  31.4 1.6 copy.73
  33.1 31.4 %reduce-scatter.3.cloned.1.call-done = bf16[24,24,2,64]{3,1,2,0:T(8,128)(2,1)} async-done(((bf16[96,24,2,64]{3,1,2,0:T(8,128)(2,1)}), bf16[24,24,2,64]{3,1,2,0:T(8,128)(2,1)}) %reduce-scatter.3.cloned.1.call-update) | async-done | bytes 147472 | tf_op jit(solution)/shard_map/reduce_scatter | solution.py:130
  64.5 1.0 copy.74
  65.8 0.9 reshape.154
  66.7 4.6 %all-to-all-start = ((bf16[8,2,4608]{2,1,0:T(2,128)(2,1)}), bf16[8,2,4608]{2,1,0:T(2,128)(2,1)S(1)}, u32[]{:S(2)}, u32[]{:S(2)}) async-start(bf16[8,2,4608]{2,1,0:T(2,128)(2,1)} %reshape.154), calls=%async_computation.1 | async-start | bytes 294912 | tf_op jit(solution)/shard_map/all_to_all | solution.py:139
  71.3 0.6 reduce-scatter.5.cloned.1.call-start
  71.8 20.8 %reshape.123 = bf16[72,24,32,64]{3,2,1,0:T(8,128)(2,1)} reshape(bf16[72,24,2048]{2,1,0:T(8,128)(2,1)} %param.7) | data formatting | bytes 14155776 | tf_op jit(solution)/shard_map/reshape | solution.py:115
  93.4 0.6 convolution_bitcast_fusion.6
  94.0 0.6 convolution_bitcast_fusion.7
  95.3 34.3 %fusion.2 = (f32[72,24,32]{2,1,0:T(8,128)}, f32[72,24,32]{2,1,0:T(8,128)}, f32[72,24,32]{2,1,0:T(8,128)}, f32[72,24,32]{2,1,0:T(8,128)S(1)}) fusion(f32[72,24,32]{2,1,0:T(8,128)S(1)} %copy.146, bf16[72,24,32,64]{3,2,1,0:T(8,128)(2,1)} %reshape.123, f32[72,24,32]{2,1,0:T(8,128)S(1)} %copy.145), kind=kLoop, calls=%fused_computation.10 | loop fusion | flops 17473536 | bytes 8404992
  129.7 2.3 copy.111
  131.9 2.2 copy.119
  134.1 2.2 copy.115
  136.3 1.0 copy.107
  137.3 1.2 add.210
  138.5 1.2 sub.98
  139.7 0.6 convolution_bitcast_fusion.12
  140.3 0.6 convolution_bitcast_fusion.13
  141.1 14.6 %all_to_all.66 = bf16[72,16,64]{0,2,1:T(8,128)(2,1)S(1)} all-to-all(bf16[72,16,64]{0,2,1:T(8,128)(2,1)S(1)} %copy.78), channel_id=1, replica_groups=mesh['gx'=4,'gy'=8] {'gy'}, dimensions={1} | all-to-all | bytes 294912 | tf_op jit(solution)/shard_map/all_to_all | solution.py:144
  155.7 0.9 copy.79
  156.6 1.4 copy.80
  158.0 38.1 %all_gather.6 = bf16[96,24,2,64]{1,0,3,2:T(8,128)(2,1)S(1)} all-gather(bf16[24,24,2,64]{1,0,3,2:T(8,128)(2,1)S(1)} %copy.80), channel_id=1, replica_groups=mesh['gx'=4,'gy'=8] {'gx'}, dimensions={0}, use_global_device_ids=true | all-gather | bytes 737280 | tf_op jit(solution)/shard_map/all_gather | solution.py:149
  196.1 5.8 %convolution_bitcast_fusion.16 = f32[96,4,2,64]{0,1,3,2:T(4,128)S(1)} fusion(bf16[96,24,2,64]{1,0,3,2:T(8,128)(2,1)S(1)} %all_gather.6, s32[24]{0:T(128)S(1)} %compare_select_fusion.2, s32[4]{0:T(128)S(1)} %iota_add_fusion), kind=kOutput, calls=%fused_computation.44 | convolution fusion | flops 14157120 | bytes 786544 | tf_op jit(solution)/shard_map/rkyc,xk->rxyc/dot_general | solution.py:43
  201.9 5.8 %convolution_bitcast_fusion.17 = f32[96,4,2,64]{0,1,3,2:T(4,128)S(1)} fusion(bf16[96,24,2,64]{1,0,3,2:T(8,128)(2,1)S(1)} %all_gather.6, s32[24]{0:T(128)S(1)} %compare_select_fusion.2, s32[4]{0:T(128)S(1)} %iota_add_fusion), kind=kOutput, calls=%fused_computation.45 | convolution fusion | flops 14157120 | bytes 786544 | tf_op jit(solution)/shard_map/rkyc,xk->rxyc/dot_general | solution.py:42
  208.1 0.4 fusion.50
  208.5 0.4 fusion.10
  208.9 2.4 fusion.22
  212.1 1.0 convolution_bitcast_fusion
  213.1 1.0 convolution_bitcast_fusion.1
  214.4 1.7 copy.86
  216.1 27.9 %reduce-scatter.5.cloned.1.call-done = bf16[24,24,2,64]{3,1,2,0:T(8,128)(2,1)} async-done(((bf16[96,24,2,64]{3,1,2,0:T(8,128)(2,1)}), bf16[24,24,2,64]{3,1,2,0:T(8,128)(2,1)}) %reduce-scatter.5.cloned.1.call-update) | async-done | bytes 147472 | tf_op jit(solution)/shard_map/reduce_scatter | solution.py:130
  244.0 1.0 copy.87
  245.5 11.6 %all_to_all.67 = bf16[8,2,4608]{2,1,0:T(2,128)(2,1)S(1)} all-to-all(bf16[8,2,4608]{2,1,0:T(2,128)(2,1)S(1)} %reshape.156), channel_id=1, replica_groups=mesh['gx'=4,'gy'=8] {'gy'}, dimensions={0} | all-to-all | bytes 294912 | tf_op jit(solution)/shard_map/all_to_all | solution.py:139
  257.8 0.6 convolution_bitcast_fusion.4
  258.4 0.6 convolution_bitcast_fusion.5
  259.0 1.0 slice_add_fusion.2
  259.9 1.3 copy.147
  261.3 2.3 copy.148
  263.6 38.7 %fusion.6 = (f32[72,24,32]{2,1,0:T(8,128)}, f32[72,24,32]{2,1,0:T(8,128)}, f32[72,24,32]{2,1,0:T(8,128)}, f32[72,24,32]{2,1,0:T(8,128)}) fusion(f32[72,24,32]{2,1,0:T(8,128)} %copy.148, bf16[72,24,32,64]{3,2,1,0:T(8,128)(2,1)} %reshape.123, f32[72,24,32]{2,1,0:T(8,128)S(1)} %copy.147), kind=kLoop, calls=%fused_computation.14 | loop fusion | flops 17473536 | bytes 8404992
  302.3 2.2 copy.131
  304.4 2.2 copy.136
  306.6 2.2 copy.141
  308.8 2.2 copy.126
  311.0 1.2 sub.104
  312.2 1.2 add.216
  313.4 0.6 convolution_bitcast_fusion.9
  314.0 0.6 convolution_bitcast_fusion.10
  314.6 20.0 %multiply_add_fusion = (f32[72,24,32,32]{3,2,1,0:T(8,128)}, f32[72,24,32,32]{3,2,1,0:T(8,128)}) fusion(f32[72,24,32]{2,1,0:T(8,128)S(1)} %copy.146, f32[72,24,32]{2,1,0:T(8,128)S(1)} %copy.145, f32[72,24,32]{2,1,0:T(8,128)} %copy.148, f32[72,24,32]{2,1,0:T(8,128)S(1)} %copy.147), kind=kLoop, calls=%fused_computation.18 | loop fusion | flops 10616832 | bytes 15040512 | tf_op jit(solution)/shard_map/add | solution.py:103
  334.7 0.8 copy.91
  335.5 3.7 all-to-all-start.3
  339.2 28.5 %pad_maximum_fusion = f32[72,24,32,64]{3,2,1,0:T(8,128)} fusion(f32[72,24,32,32]{3,2,1,0:T(8,128)} %get-tuple-element.15, f32[72,24,32,32]{3,2,1,0:T(8,128)} %get-tuple-element.14), kind=kLoop, calls=%fused_computation.16 | loop fusion | flops 3538944 | bytes 28311552 | tf_op jit(solution)/shard_map/concatenate | solution.py:105
  367.7 24.3 %reshape.127 = f32[72,24,2048]{2,1,0:T(8,128)} reshape(f32[72,24,32,64]{3,2,1,0:T(8,128)} %pad_maximum_fusion) | data formatting | bytes 28311552 | tf_op jit(solution)/shard_map/reshape | solution.py:168
  392.2 0.4 copy.93
  392.7 40.0 %all_gather.7 = bf16[96,24,2,64]{1,0,3,2:T(8,128)(2,1)S(1)} all-gather(bf16[24,24,2,64]{1,0,3,2:T(8,128)(2,1)S(1)} %copy.93), channel_id=1, replica_groups=mesh['gx'=4,'gy'=8] {'gx'}, dimensions={0}, use_global_device_ids=true | all-gather | bytes 737280 | tf_op jit(solution)/shard_map/all_gather | solution.py:149
  432.7 5.8 %convolution_bitcast_fusion.14 = f32[96,4,2,64]{0,1,3,2:T(4,128)S(1)} fusion(bf16[96,24,2,64]{1,0,3,2:T(8,128)(2,1)S(1)} %all_gather.7, s32[24]{0:T(128)S(1)} %compare_select_fusion.2, s32[4]{0:T(128)S(1)} %iota_add_fusion), kind=kOutput, calls=%fused_computation.42 | convolution fusion | flops 14157120 | bytes 786544 | tf_op jit(solution)/shard_map/rkyc,xk->rxyc/dot_general | solution.py:43
  438.5 5.8 %convolution_bitcast_fusion.15 = f32[96,4,2,64]{0,1,3,2:T(4,128)S(1)} fusion(bf16[96,24,2,64]{1,0,3,2:T(8,128)(2,1)S(1)} %all_gather.7, s32[24]{0:T(128)S(1)} %compare_select_fusion.2, s32[4]{0:T(128)S(1)} %iota_add_fusion), kind=kOutput, calls=%fused_computation.43 | convolution fusion | flops 14157120 | bytes 786544 | tf_op jit(solution)/shard_map/rkyc,xk->rxyc/dot_general | solution.py:42
  445.4 0.9 fusion.12
  (59 shorter events, 6.6 us)
Async XLA Ops:
  7.2 19.3 %copy-start = (bf16[4,2,32,512]{3,2,1,0:T(8,128)(2,1)S(1)}, bf16[4,2,32,512]{3,2,1,0:T(8,128)(2,1)}, u32[]{:S(2)}) copy-start(bf16[4,2,32,512]{3,2,1,0:T(8,128)(2,1)} %param.4) | copy-start | bytes 786436
  7.2 57.3 %reduce-scatter.3.cloned.1.call-start = ((), (), s32[]{:S(2)}) async-start(), calls=%async_computation.6 | async-start | bytes 1474560 | tf_op jit(solution)/shard_map/reduce_scatter | solution.py:130
  66.7 26.0 %all-to-all-start = ((bf16[8,2,4608]{2,1,0:T(2,128)(2,1)}), bf16[8,2,4608]{2,1,0:T(2,128)(2,1)S(1)}, u32[]{:S(2)}, u32[]{:S(2)}) async-start(bf16[8,2,4608]{2,1,0:T(2,128)(2,1)} %reshape.154), calls=%async_computation.1 | async-start | bytes 294912 | tf_op jit(solution)/shard_map/all_to_all | solution.py:139
  71.3 172.7 %reduce-scatter.5.cloned.1.call-start = ((), (), s32[]{:S(2)}) async-start(), calls=%async_computation.7 | async-start | bytes 1474560 | tf_op jit(solution)/shard_map/reduce_scatter | solution.py:130
  129.6 78.4 %copy-start.3 = (f32[512,96,1,1]{0,1,2,3:T(8,128)S(1)}, f32[512,96,1,1]{0,1,2,3:T(8,128)}, u32[]{:S(2)}) copy-start(f32[512,96,1,1]{0,1,2,3:T(8,128)} %reshape.128) | copy-start | bytes 589828
  129.7 78.8 %copy-start.2 = (f32[512,96,1,1]{0,1,2,3:T(8,128)S(1)}, f32[512,96,1,1]{0,1,2,3:T(8,128)}, u32[]{:S(2)}) copy-start(f32[512,96,1,1]{0,1,2,3:T(8,128)} %reshape.129) | copy-start | bytes 589828
  129.7 79.2 %copy-start.6 = (bf16[32,32]{1,0:T(8,128)(2,1)S(1)}, bf16[32,32]{1,0:T(8,128)(2,1)}, u32[]{:S(2)}) copy-start(bf16[32,32]{1,0:T(8,128)(2,1)} %param.6) | copy-start | bytes 6148
  211.2 3.0 copy-start.4
  335.5 56.5 %all-to-all-start.3 = ((bf16[72,16,64]{0,2,1:T(8,128)(2,1)}), bf16[72,16,64]{0,2,1:T(8,128)(2,1)S(1)}, u32[]{:S(2)}, u32[]{:S(2)}) async-start(bf16[72,16,64]{0,2,1:T(8,128)(2,1)} %copy.91), calls=%async_computation.5 | async-start | bytes 524288 | tf_op jit(solution)/shard_map/all_to_all | solution.py:144
  367.7 78.6 %copy-start.1 = (bf16[4,2,32,512]{3,2,1,0:T(8,128)(2,1)S(1)}, bf16[4,2,32,512]{3,2,1,0:T(8,128)(2,1)}, u32[]{:S(2)}) copy-start(bf16[4,2,32,512]{3,2,1,0:T(8,128)(2,1)} %param.4) | copy-start | bytes 786436
  392.0 53.4 %copy-start.5 = (bf16[4,2,32,512]{3,2,1,0:T(8,128)(2,1)S(1)}, bf16[4,2,32,512]{3,2,1,0:T(8,128)(2,1)}, u32[]{:S(2)}) copy-start(bf16[4,2,32,512]{3,2,1,0:T(8,128)(2,1)} %copy-done.4) | copy-start | bytes 786436
Sparse Core Ops, SparseCore 0:
  33.2 31.2 reduce-scatter.2
  216.2 27.7 reduce-scatter.4
where the time goes:
time: 463 us; the launch traced here: 454 us
  other arithmetic  141 us (30%)
  blocking collectives  104 us (22%)
  local copies, waits for them, and re-layouts  84.9 us (18%)
  waiting for transfers between devices  59.4 us (13%)
  matrix products  40.2 us (9%)
  between operations  15 us (3%)
  starting transfers between devices  8.86 us (2%)
    all_gather x2, blocking collectives, to_space(): lax.all_gather(returned, 'gx', axis=0, tiled=True).astype(jnp.float32)  78.1 us
    unnamed x2, other arithmetic  73 us
    reduce_scatter x2, waiting for transfers between devices, to_modes(): lax.psum_scatter(rotate(depth_spec.astype(jnp.float32), local_x[0], local...  59.3 us
    concatenate x1, other arithmetic, weight_grad(): return jnp.concatenate([real_part, imag_part], -1)  28.5 us
    reshape x1, local copies, waits for them, and re-layouts, per_device(): weight_grad(spectra_in, spectra_back)  24.3 us
    reshape x1, local copies, waits for them, and re-layouts, per_device(): spectral_weight.reshape(mode_rows, mode_cols, channels, 2 * channels)  20.8 us
    add x1, other arithmetic, weight_grad(): partial_outer(real_in, real_back) + partial_outer(imag_in, imag_back)  20 us
    dot_general x8, matrix products, rotate(): jnp.einsum(pattern, spectra, cosine_table, precision=lax.Precision.HIGHEST)  16 us
  transfers between devices with their start and end apart: 4, of which 2 were waited for; matrix products, arithmetic and copies ran while one was open for 16% of the time, Pallas kernels for 0%

commit v1 on v0

--- a/solution.py
+++ b/solution.py
@@ -10,6 +10,18 @@
 KY = 24
 KZ = 12
 KT = 8
+
+
+def _shape_record(payload, which_dim, panel):
+    seen_now, outer = (payload.shape[:which_dim], payload.shape[which_dim + 1 :])
+    top = payload.reshape(*seen_now, panel, -1, *outer)
+    return jnp.moveaxis(top, which_dim, 0)
+
+
+def cover_figure(message, d0):
+    message = jnp.moveaxis(message, 0, d0)
+    v_next = message.shape
+    return message.reshape(*v_next[:d0], v_next[d0] * v_next[d0 + 1], *v_next[d0 + 2 :])
 
 
 def kept_angles(positions, kept_count, length):
@@ -141,7 +153,22 @@
 
     def to_space(spectra, factor):
         back_rows = settle(rotate(spectra, whole_y[0], whole_y[1], "mkc,yk->myc", -1.0))
-        returned = lax.all_to_all(back_rows, "gy", split_axis=1, concat_axis=0, tiled=True)
+        met_up = lax.axis_size("gy")
+        local_out = lax.axis_index("gy")
+        all_rows, mid_arr = (met_up, local_out)
+        main = _shape_record(back_rows, 1, all_rows)
+        line_up = [main[mid_arr]]
+        for src_i in range(1, all_rows):
+            block_last = main[(mid_arr + src_i) % all_rows]
+            w2 = lax.ppermute(
+                block_last,
+                axis_name="gy",
+                perm=[(w, (w + src_i) % all_rows) for w in range(all_rows)],
+            )
+            line_up.append(w2)
+        known = jnp.stack(line_up, 0)
+        main = known[(mid_arr - jnp.arange(all_rows)) % all_rows]
+        returned = cover_figure(main, 0)
         share = returned.shape[0] // KX
         returned = returned.reshape(share, KX, rows_y, 2 * channels)
         back_depth = settle(

time: 463 us -> 464 us (level)
  starting transfers between devices: 8.86 us -> 22.3 us
  blocking collectives: 104 us -> 93.2 us
  other arithmetic: 141 us -> 135 us
    ppermute x0 -> x14, starting transfers between devices: none -> 17.5 us  [to_space(): lax.ppermute(block_last, axis_name='gy', perm=[(w, (w + src_i) % all_rows...]
    all_to_all x1 -> x0, blocking collectives: 14.6 us -> none  [to_space(): lax.all_to_all(back_rows, 'gy', split_axis=1, concat_axis=0, tiled=True)]
    concatenate x1, other arithmetic: 28.5 us -> 22.3 us  [weight_grad(): return jnp.concatenate([real_part, imag_part], -1)]
  transfers between devices with their start and end apart: 4 -> 17, of which waited for: 2 -> 7; matrix products, arithmetic and copies ran while one was open for 16% -> 15% of each run, Pallas kernels for 0% -> 0%
where the time goes in v1:
time: 464 us; the launch traced here: 455 us
  other arithmetic  135 us (29%)
  blocking collectives  93.2 us (20%)
  local copies, waits for them, and re-layouts  86 us (19%)
  waiting for transfers between devices  63 us (14%)
  matrix products  40.2 us (9%)
  starting transfers between devices  22.3 us (5%)
  between operations  15.1 us (3%)
    all_gather x2, blocking collectives, to_space(): lax.all_gather(returned, 'gx', axis=0, tiled=True).astype(jnp.float32)  81.4 us
    unnamed x2, other arithmetic  73 us
    reduce_scatter x2, waiting for transfers between devices, to_modes(): lax.psum_scatter(rotate(depth_spec.astype(jnp.float32), local_x[0], local...  59.9 us
    reshape x1, local copies, waits for them, and re-layouts, per_device(): weight_grad(spectra_in, spectra_back)  24.3 us
    concatenate x1, other arithmetic, weight_grad(): return jnp.concatenate([real_part, imag_part], -1)  22.3 us
    reshape x1, local copies, waits for them, and re-layouts, per_device(): spectral_weight.reshape(mode_rows, mode_cols, channels, 2 * channels)  20.8 us
    add x1, other arithmetic, weight_grad(): partial_outer(real_in, real_back) + partial_outer(imag_in, imag_back)  20.4 us
    ppermute x14, starting transfers between devices, to_space(): lax.ppermute(block_last, axis_name='gy', perm=[(w, (w + src_i) % all_rows...  17.5 us
  transfers between devices with their start and end apart: 17, of which 7 were waited for; matrix products, arithmetic and copies ran while one was open for 15% of the time, Pallas kernels for 0%

profile of v1, /device:TPU:0, one launch (start us, length us, event | category | flops | bytes accessed | tf_op | source)
XLA Modules:
  0.0 455.1 jit_solution(13285788758404191739)
XLA Ops:
  7.4 12.3 %add_sine_fusion = (f32[64,8,12,8]{1,0,3,2:T(8,128)}, f32[64,8,12,8]{1,0,3,2:T(8,128)S(1)}) fusion(f32[8,8]{0,1:T(8,128)S(1)} %fusion.94, f32[64,12]{0,1:T(8,128)S(1)} %fusion.75), kind=kLoop, calls=%fused_computation.21 | loop fusion | flops 49152 | bytes 396544 | tf_op jit(solution)/shard_map/sin | solution.py:45
  19.8 3.9 reshape.222
  23.7 2.8 reshape.221
  26.5 1.3 convolution_negate_fusion.1
  27.8 1.3 fusion.52
  29.1 1.0 convolution_bitcast_fusion.2
  30.1 1.0 convolution_bitcast_fusion.3
  31.4 1.6 copy.60
  33.1 31.4 %reduce-scatter.3.cloned.1.call-done = bf16[24,24,2,64]{3,1,2,0:T(8,128)(2,1)} async-done(((bf16[96,24,2,64]{3,1,2,0:T(8,128)(2,1)}), bf16[24,24,2,64]{3,1,2,0:T(8,128)(2,1)}) %reduce-scatter.3.cloned.1.call-update) | async-done | bytes 147472 | tf_op jit(solution)/shard_map/reduce_scatter | solution.py:142
  64.5 1.0 copy.61
  65.8 0.9 reshape.247
  66.7 4.6 %all-to-all-start = ((bf16[8,2,4608]{2,1,0:T(2,128)(2,1)}), bf16[8,2,4608]{2,1,0:T(2,128)(2,1)S(1)}, u32[]{:S(2)}, u32[]{:S(2)}) async-start(bf16[8,2,4608]{2,1,0:T(2,128)(2,1)} %reshape.247), calls=%async_computation.1 | async-start | bytes 294912 | tf_op jit(solution)/shard_map/all_to_all | solution.py:151
  71.6 20.8 %reshape.200 = bf16[72,24,32,64]{3,2,1,0:T(8,128)(2,1)} reshape(bf16[72,24,2048]{2,1,0:T(8,128)(2,1)} %param.7) | data formatting | bytes 14155776 | tf_op jit(solution)/shard_map/reshape | solution.py:127
  95.1 34.4 %fusion.2 = (f32[72,24,32]{2,1,0:T(8,128)}, f32[72,24,32]{2,1,0:T(8,128)}, f32[72,24,32]{2,1,0:T(8,128)}, f32[72,24,32]{2,1,0:T(8,128)S(1)}) fusion(f32[72,24,32]{2,1,0:T(8,128)S(1)} %copy.147, bf16[72,24,32,64]{3,2,1,0:T(8,128)(2,1)} %reshape.200, f32[72,24,32]{2,1,0:T(8,128)S(1)} %copy.146), kind=kLoop, calls=%fused_computation.12 | loop fusion | flops 17473536 | bytes 8404992
  129.5 2.3 copy.112
  131.8 2.3 copy.120
  134.0 2.2 copy.116
  136.2 1.1 copy.108
  137.3 1.2 add.325
  138.4 1.2 sub.113
  140.2 0.6 convolution_bitcast_fusion.13
  141.8 1.7 collective-permute-start.1
  143.5 2.2 collective-permute-start.2
  145.7 1.5 collective-permute-start.3
  147.1 1.0 collective-permute-start.4
  148.2 1.5 collective-permute-start.5
  149.8 1.4 collective-permute-start.6
  151.3 1.0 collective-permute-done.5
  153.3 0.9 copy.73
  154.2 1.4 copy.74
  155.6 40.6 %all_gather.6 = bf16[96,24,2,64]{1,0,3,2:T(8,128)(2,1)S(1)} all-gather(bf16[24,24,2,64]{1,0,3,2:T(8,128)(2,1)S(1)} %copy.74), channel_id=1, replica_groups=mesh['gx'=4,'gy'=8] {'gx'}, dimensions={0}, use_global_device_ids=true | all-gather | bytes 737280 | tf_op jit(solution)/shard_map/all_gather | solution.py:176
  196.2 5.8 %convolution_bitcast_fusion.16 = f32[96,4,2,64]{0,1,3,2:T(4,128)S(1)} fusion(bf16[96,24,2,64]{1,0,3,2:T(8,128)(2,1)S(1)} %all_gather.6, s32[24]{0:T(128)S(1)} %compare_select_fusion.3, s32[4]{0:T(128)S(1)} %iota_add_fusion), kind=kOutput, calls=%fused_computation.46 | convolution fusion | flops 14157120 | bytes 786544 | tf_op jit(solution)/shard_map/rkyc,xk->rxyc/dot_general | solution.py:55
  202.0 5.8 %convolution_bitcast_fusion.17 = f32[96,4,2,64]{0,1,3,2:T(4,128)S(1)} fusion(bf16[96,24,2,64]{1,0,3,2:T(8,128)(2,1)S(1)} %all_gather.6, s32[24]{0:T(128)S(1)} %compare_select_fusion.3, s32[4]{0:T(128)S(1)} %iota_add_fusion), kind=kOutput, calls=%fused_computation.47 | convolution fusion | flops 14157120 | bytes 786544 | tf_op jit(solution)/shard_map/rkyc,xk->rxyc/dot_general | solution.py:54
  209.0 2.4 fusion.22
  212.2 1.0 convolution_bitcast_fusion
  213.2 1.0 convolution_bitcast_fusion.1
  214.5 1.7 copy.80
  216.2 28.5 %reduce-scatter.5.cloned.1.call-done = bf16[24,24,2,64]{3,1,2,0:T(8,128)(2,1)} async-done(((bf16[96,24,2,64]{3,1,2,0:T(8,128)(2,1)}), bf16[24,24,2,64]{3,1,2,0:T(8,128)(2,1)}) %reduce-scatter.5.cloned.1.call-update) | async-done | bytes 147472 | tf_op jit(solution)/shard_map/reduce_scatter | solution.py:142
  244.7 1.0 copy.81
  246.2 11.8 %all_to_all.36 = bf16[8,2,4608]{2,1,0:T(2,128)(2,1)S(1)} all-to-all(bf16[8,2,4608]{2,1,0:T(2,128)(2,1)S(1)} %reshape.249), channel_id=1, replica_groups=mesh['gx'=4,'gy'=8] {'gy'}, dimensions={0} | all-to-all | bytes 294912 | tf_op jit(solution)/shard_map/all_to_all | solution.py:151
  259.9 1.0 slice_add_fusion.2
  260.8 1.3 copy.148
  262.2 2.3 copy.149
  264.4 38.6 %fusion.6 = (f32[72,24,32]{2,1,0:T(8,128)}, f32[72,24,32]{2,1,0:T(8,128)}, f32[72,24,32]{2,1,0:T(8,128)}, f32[72,24,32]{2,1,0:T(8,128)}) fusion(f32[72,24,32]{2,1,0:T(8,128)} %copy.149, bf16[72,24,32,64]{3,2,1,0:T(8,128)(2,1)} %reshape.200, f32[72,24,32]{2,1,0:T(8,128)S(1)} %copy.148), kind=kLoop, calls=%fused_computation.16 | loop fusion | flops 17473536 | bytes 8404992
  303.0 2.2 copy.132
  305.2 2.2 copy.137
  307.4 2.2 copy.142
  309.7 2.2 copy.127
  311.9 1.2 sub.121
  313.1 1.2 add.355
  314.8 0.6 convolution_bitcast_fusion.10
  315.5 20.4 %multiply_add_fusion = (f32[72,24,32,32]{3,2,1,0:T(8,128)S(1)}, f32[72,24,32,32]{3,2,1,0:T(8,128)}) fusion(f32[72,24,32]{2,1,0:T(8,128)S(1)} %copy.147, f32[72,24,32]{2,1,0:T(8,128)S(1)} %copy.146, f32[72,24,32]{2,1,0:T(8,128)} %copy.149, f32[72,24,32]{2,1,0:T(8,128)S(1)} %copy.148), kind=kLoop, calls=%fused_computation.20 | loop fusion | flops 10616832 | bytes 15040512 | tf_op jit(solution)/shard_map/add | solution.py:115
  336.4 1.0 collective-permute-start.8
  337.4 1.1 collective-permute-start.9
  338.5 2.7 collective-permute-start.10
  341.3 22.3 %pad_maximum_fusion = f32[72,24,32,64]{3,2,1,0:T(8,128)} fusion(f32[72,24,32,32]{3,2,1,0:T(8,128)} %get-tuple-element.15, f32[72,24,32,32]{3,2,1,0:T(8,128)S(1)} %get-tuple-element.14), kind=kLoop, calls=%fused_computation.18 | loop fusion | flops 3538944 | bytes 28311552 | tf_op jit(solution)/shard_map/concatenate | solution.py:117
  363.7 24.3 %reshape.204 = f32[72,24,2048]{2,1,0:T(8,128)} reshape(f32[72,24,32,64]{3,2,1,0:T(8,128)} %pad_maximum_fusion) | data formatting | bytes 28311552 | tf_op jit(solution)/shard_map/reshape | solution.py:195
  388.0 2.1 collective-permute-start.12
  390.1 0.6 collective-permute-start.13
  390.8 1.1 collective-permute-done.12
  393.6 40.8 %all_gather.7 = bf16[96,24,2,64]{1,0,3,2:T(8,128)(2,1)S(1)} all-gather(bf16[24,24,2,64]{1,0,3,2:T(8,128)(2,1)S(1)} %copy.94), channel_id=1, replica_groups=mesh['gx'=4,'gy'=8] {'gx'}, dimensions={0}, use_global_device_ids=true | all-gather | bytes 737280 | tf_op jit(solution)/shard_map/all_gather | solution.py:176
  434.4 5.8 %convolution_bitcast_fusion.14 = f32[96,4,2,64]{0,1,3,2:T(4,128)S(1)} fusion(bf16[96,24,2,64]{1,0,3,2:T(8,128)(2,1)S(1)} %all_gather.7, s32[24]{0:T(128)S(1)} %compare_select_fusion.3, s32[4]{0:T(128)S(1)} %iota_add_fusion), kind=kOutput, calls=%fused_computation.44 | convolution fusion | flops 14157120 | bytes 786544 | tf_op jit(solution)/shard_map/rkyc,xk->rxyc/dot_general | solution.py:55
  440.2 5.8 %convolution_bitcast_fusion.15 = f32[96,4,2,64]{0,1,3,2:T(4,128)S(1)} fusion(bf16[96,24,2,64]{1,0,3,2:T(8,128)(2,1)S(1)} %all_gather.7, s32[24]{0:T(128)S(1)} %compare_select_fusion.3, s32[4]{0:T(128)S(1)} %iota_add_fusion), kind=kOutput, calls=%fused_computation.45 | convolution fusion | flops 14157120 | bytes 786544 | tf_op jit(solution)/shard_map/rkyc,xk->rxyc/dot_general | solution.py:54
  447.1 0.9 fusion.12
  (118 shorter events, 14.9 us)
Async XLA Ops:
  7.2 19.3 %copy-start = (bf16[4,2,32,512]{3,2,1,0:T(8,128)(2,1)S(1)}, bf16[4,2,32,512]{3,2,1,0:T(8,128)(2,1)}, u32[]{:S(2)}) copy-start(bf16[4,2,32,512]{3,2,1,0:T(8,128)(2,1)} %param.4) | copy-start | bytes 786436
  7.2 57.3 %reduce-scatter.3.cloned.1.call-start = ((), (), s32[]{:S(2)}) async-start(), calls=%async_computation.4 | async-start | bytes 1474560 | tf_op jit(solution)/shard_map/reduce_scatter | solution.py:142
  66.7 25.8 %all-to-all-start = ((bf16[8,2,4608]{2,1,0:T(2,128)(2,1)}), bf16[8,2,4608]{2,1,0:T(2,128)(2,1)S(1)}, u32[]{:S(2)}, u32[]{:S(2)}) async-start(bf16[8,2,4608]{2,1,0:T(2,128)(2,1)} %reshape.247), calls=%async_computation.1 | async-start | bytes 294912 | tf_op jit(solution)/shard_map/all_to_all | solution.py:151
  71.3 173.4 %reduce-scatter.5.cloned.1.call-start = ((), (), s32[]{:S(2)}) async-start(), calls=%async_computation.5 | async-start | bytes 1474560 | tf_op jit(solution)/shard_map/reduce_scatter | solution.py:142
  129.5 78.7 %copy-start.3 = (f32[512,96,1,1]{0,1,2,3:T(8,128)S(1)}, f32[512,96,1,1]{0,1,2,3:T(8,128)}, u32[]{:S(2)}) copy-start(f32[512,96,1,1]{0,1,2,3:T(8,128)} %reshape.221) | copy-start | bytes 589828
  129.5 79.1 %copy-start.2 = (f32[512,96,1,1]{0,1,2,3:T(8,128)S(1)}, f32[512,96,1,1]{0,1,2,3:T(8,128)}, u32[]{:S(2)}) copy-start(f32[512,96,1,1]{0,1,2,3:T(8,128)} %reshape.222) | copy-start | bytes 589828
  131.8 77.2 %copy-start.6 = (bf16[32,32]{1,0:T(8,128)(2,1)S(1)}, bf16[32,32]{1,0:T(8,128)(2,1)}, u32[]{:S(2)}) copy-start(bf16[32,32]{1,0:T(8,128)(2,1)} %param.6) | copy-start | bytes 6148
  141.3 6.9 %collective-permute-start = (bf16[72,2,64]{0,2,1:T(8,128)(2,1)S(1)}, bf16[72,2,64]{0,2,1:T(8,128)(2,1)S(1)}, u32[]{:S(2)}, u32[]{:S(2)}) collective-permute-start(bf16[72,2,64]{0,2,1:T(8,128)(2,1)S(1)} %bitcast.257), channel_id=1, source_target_pairs={{0,1},{1,2},{2,3},{3,4},{4,5},{5,6},{6,7},{7,0},{8,9},{9,10},{10,1... | collective-permute-start | bytes 55304 | tf_op jit(solution)/shard_map/ppermute | solution.py:163
  141.8 8.0 %collective-permute-start.1 = (bf16[72,2,64]{0,2,1:T(8,128)(2,1)S(1)}, bf16[72,2,64]{0,2,1:T(8,128)(2,1)S(1)}, u32[]{:S(2)}, u32[]{:S(2)}) collective-permute-start(bf16[72,2,64]{0,2,1:T(8,128)(2,1)S(1)} %bitcast.255), channel_id=1, source_target_pairs={{0,2},{1,3},{2,4},{3,5},{4,6},{5,7},{6,0},{7,1},{8,10},{9,11},{10,... | collective-permute-start | bytes 55304 | tf_op jit(solution)/shard_map/ppermute | solution.py:163
  143.5 7.7 %collective-permute-start.2 = (bf16[72,2,64]{0,2,1:T(8,128)(2,1)S(1)}, bf16[72,2,64]{0,2,1:T(8,128)(2,1)S(1)}, u32[]{:S(2)}, u32[]{:S(2)}) collective-permute-start(bf16[72,2,64]{0,2,1:T(8,128)(2,1)S(1)} %bitcast.250), channel_id=1, source_target_pairs={{0,3},{1,4},{2,5},{3,6},{4,7},{5,0},{6,1},{7,2},{8,11},{9,12},{10,... | collective-permute-start | bytes 55304 | tf_op jit(solution)/shard_map/ppermute | solution.py:163
  145.7 5.5 %collective-permute-start.3 = (bf16[72,2,64]{0,2,1:T(8,128)(2,1)S(1)}, bf16[72,2,64]{0,2,1:T(8,128)(2,1)S(1)}, u32[]{:S(2)}, u32[]{:S(2)}) collective-permute-start(bf16[72,2,64]{0,2,1:T(8,128)(2,1)S(1)} %bitcast.247), channel_id=1, source_target_pairs={{0,4},{1,5},{2,6},{3,7},{4,0},{5,1},{6,2},{7,3},{8,12},{9,13},{10,... | collective-permute-start | bytes 55304 | tf_op jit(solution)/shard_map/ppermute | solution.py:163
  147.1 4.1 collective-permute-start.4
  148.2 4.0 collective-permute-start.5
  149.8 3.0 collective-permute-start.6
  211.4 3.0 copy-start.4
  336.3 51.7 %collective-permute-start.7 = (bf16[72,2,64]{0,2,1:T(8,128)(2,1)S(1)}, bf16[72,2,64]{0,2,1:T(8,128)(2,1)S(1)}, u32[]{:S(2)}, u32[]{:S(2)}) collective-permute-start(bf16[72,2,64]{0,2,1:T(8,128)(2,1)S(1)} %bitcast.256), channel_id=1, source_target_pairs={{0,1},{1,2},{2,3},{3,4},{4,5},{5,6},{6,7},{7,0},{8,9},{9,10},{10,1... | collective-permute-start | bytes 55304 | tf_op jit(solution)/shard_map/ppermute | solution.py:163
  336.4 53.7 %collective-permute-start.8 = (bf16[72,2,64]{0,2,1:T(8,128)(2,1)S(1)}, bf16[72,2,64]{0,2,1:T(8,128)(2,1)S(1)}, u32[]{:S(2)}, u32[]{:S(2)}) collective-permute-start(bf16[72,2,64]{0,2,1:T(8,128)(2,1)S(1)} %bitcast.252), channel_id=1, source_target_pairs={{0,2},{1,3},{2,4},{3,5},{4,6},{5,7},{6,0},{7,1},{8,10},{9,11},{10,... | collective-permute-start | bytes 55304 | tf_op jit(solution)/shard_map/ppermute | solution.py:163
  337.4 53.3 %collective-permute-start.9 = (bf16[72,2,64]{0,2,1:T(8,128)(2,1)S(1)}, bf16[72,2,64]{0,2,1:T(8,128)(2,1)S(1)}, u32[]{:S(2)}, u32[]{:S(2)}) collective-permute-start(bf16[72,2,64]{0,2,1:T(8,128)(2,1)S(1)} %bitcast.248), channel_id=1, source_target_pairs={{0,3},{1,4},{2,5},{3,6},{4,7},{5,0},{6,1},{7,2},{8,11},{9,12},{10,... | collective-permute-start | bytes 55304 | tf_op jit(solution)/shard_map/ppermute | solution.py:163
  338.5 52.3 %collective-permute-start.10 = (bf16[72,2,64]{0,2,1:T(8,128)(2,1)S(1)}, bf16[72,2,64]{0,2,1:T(8,128)(2,1)S(1)}, u32[]{:S(2)}, u32[]{:S(2)}) collective-permute-start(bf16[72,2,64]{0,2,1:T(8,128)(2,1)S(1)} %bitcast.246), channel_id=1, source_target_pairs={{0,4},{1,5},{2,6},{3,7},{4,0},{5,1},{6,2},{7,3},{8,12},{9,13},{10,... | collective-permute-start | bytes 55304 | tf_op jit(solution)/shard_map/ppermute | solution.py:163
  341.2 49.6 %collective-permute-start.11 = (bf16[72,2,64]{0,2,1:T(8,128)(2,1)S(1)}, bf16[72,2,64]{0,2,1:T(8,128)(2,1)S(1)}, u32[]{:S(2)}, u32[]{:S(2)}) collective-permute-start(bf16[72,2,64]{0,2,1:T(8,128)(2,1)S(1)} %bitcast.244), channel_id=1, source_target_pairs={{0,5},{1,6},{2,7},{3,0},{4,1},{5,2},{6,3},{7,4},{8,13},{9,14},{10,... | collective-permute-start | bytes 55304 | tf_op jit(solution)/shard_map/ppermute | solution.py:163
  363.7 84.4 %copy-start.1 = (bf16[4,2,32,512]{3,2,1,0:T(8,128)(2,1)S(1)}, bf16[4,2,32,512]{3,2,1,0:T(8,128)(2,1)}, u32[]{:S(2)}) copy-start(bf16[4,2,32,512]{3,2,1,0:T(8,128)(2,1)} %param.4) | copy-start | bytes 786436
  388.0 59.1 %copy-start.5 = (bf16[4,2,32,512]{3,2,1,0:T(8,128)(2,1)S(1)}, bf16[4,2,32,512]{3,2,1,0:T(8,128)(2,1)}, u32[]{:S(2)}) copy-start(bf16[4,2,32,512]{3,2,1,0:T(8,128)(2,1)} %copy-done.4) | copy-start | bytes 786436
  388.0 3.9 collective-permute-start.12
  390.1 2.2 collective-permute-start.13
Sparse Core Ops, SparseCore 0:
  33.2 31.2 reduce-scatter.2
  216.3 28.3 reduce-scatter.4
